TPU v7x, 128 devices: a whole 4x4x4 slice. The times are simulated.
128 devices in a mesh: frame: 16 (over y, x), tensor: 8 (over z, core).
Axes of the slice: x: 4, y: 4, z: 4, core: 2. Of those that a mesh axis runs over, the one named last changes fastest.
Arguments:
- latents: bfloat16 [8192, 5120], P('frame', 'tensor'), may hold values from -6 to 6
- w_query: bfloat16 [5120, 3072], P(None, 'tensor'), may hold values from -0.078125 to 0.078125
- w_key: bfloat16 [5120, 3072], P(None, 'tensor'), may hold values from -0.078125 to 0.078125
- w_value: bfloat16 [5120, 3072], P(None, 'tensor'), may hold values from -0.078125 to 0.078125
- w_out: bfloat16 [3072, 5120], P('tensor'), may hold values from -0.109375 to 0.109375
- query_gain: float32 [24, 128], P('tensor'), may hold values from 0.5 to 14, as said below
- key_gain: float32 [24, 128], P('tensor'), may hold values from 0.5 to 14, as said below
- mod_table: float32 [16, 3, 5120], replicated, may hold values from -3 to 3
- levels: int32 [16], P('frame'), may hold values from 0 to 15
- span_counts: int32 [16], replicated, may hold values from 1 to 512, 6144 in all
- block_mask: int32 [16, 16], P('frame'), may hold values 0 or 1
- span_order: int32 [16], replicated, may hold values from 0 to 15, each once
Outputs:
- updated: bfloat16 [8192, 5120], P('frame', 'tensor')
Inputs may be any that keep to these rules, and one draw needn't show every extreme that they name: `query_gain`: gains are positive. `key_gain`: gains are positive. `span_order`: each rank appears once.
All inputs are finite; a program needn't handle non-finite values. No bound on the sum of `block_mask` on one device may be relied on, other than what follows from the above.
Results may differ from a plain program's by a relative error of at most 0.012.
The roundings to bfloat16 on the way count: a program that leaves them out, or rounds other values in their place, can miss the bound.
Values may be sent and summed in bfloat16 or wider, within the bound.
No kernel may reach another device: no remote copies, remote signals or barrier semaphores. Data moves between devices by JAX's collectives and lax.ppermute only.
A program may use at most 128 MiB of HBM per device.

v0:
```python
import math
import jax
import jax.numpy as jnp
from jax import lax
from jax.sharding import PartitionSpec as P

HEAD_DIM = 128
EPSILON = 1e-06
NEG_FILL = -1e30


def on_device(
    latents,
    w_query,
    w_key,
    w_value,
    w_out,
    query_gain,
    key_gain,
    mod_table,
    levels,
    span_counts,
    block_mask,
    span_order,
):
    row_count = latents.shape[0]
    shard_width = latents.shape[1]
    span_total = lax.axis_size("frame")
    my_span = lax.axis_index("frame")
    column_start = lax.axis_index("tensor") * shard_width
    selector = jnp.arange(mod_table.shape[0], dtype=jnp.int32) == levels[0]
    modulation = jnp.sum(jnp.where(selector[:, None, None], mod_table, 0.0), axis=0)
    shift_row = modulation[0]
    scale_row = modulation[1]
    gate_row = modulation[2]
    whole = lax.all_gather(latents, "tensor", axis=1, tiled=True).astype(jnp.float32)
    row_mean = jnp.mean(whole, axis=1, keepdims=True)
    row_square = jnp.mean(whole * whole, axis=1, keepdims=True)
    normed = (
        (whole - row_mean)
        * lax.rsqrt(row_square - row_mean * row_mean + EPSILON)
        * (1.0 + scale_row)
        + shift_row
    ).astype(jnp.bfloat16)
    head_local = w_query.shape[1] // HEAD_DIM

    def project(weight, gain_table):
        shaped = jnp.dot(normed, weight, preferred_element_type=jnp.float32).reshape(
            row_count, head_local, HEAD_DIM
        )
        scaled = (
            shaped
            * lax.rsqrt(jnp.mean(shaped * shaped, axis=-1, keepdims=True) + EPSILON)
            * gain_table
        )
        return scaled.astype(jnp.bfloat16)

    queries = project(w_query, query_gain)
    keys_local = project(w_key, key_gain).reshape(row_count, head_local * HEAD_DIM)
    values_local = jnp.dot(normed, w_value, preferred_element_type=jnp.float32).astype(jnp.bfloat16)
    kv_pair = jnp.stack((keys_local, values_local))
    span_ids = jnp.arange(span_total, dtype=jnp.int32)
    my_rank = jnp.sum(jnp.where(span_ids == my_span, span_order, 0))
    mask_row = block_mask[0]
    slot_index = jnp.arange(row_count, dtype=jnp.int32)
    score_factor = 1.0 / math.sqrt(HEAD_DIM)
    initial = (
        jnp.full((head_local, row_count), NEG_FILL, jnp.float32),
        jnp.zeros((head_local, row_count), jnp.float32),
        jnp.zeros((head_local, row_count, HEAD_DIM), jnp.float32),
    )
    piece = lax.all_gather(kv_pair, "frame", axis=1, tiled=True)
    block_count = piece.shape[1] // row_count
    key_blocks = piece[0].reshape(block_count, row_count, head_local, HEAD_DIM)
    value_blocks = piece[1].reshape(block_count, row_count, head_local, HEAD_DIM)

    def fold_block(running, block):
        key_block, value_block, block_index = block
        source_count = jnp.sum(jnp.where(span_ids == block_index, span_counts, 0))
        linked = jnp.sum(jnp.where(span_ids == block_index, mask_row, 0)) == 1
        source_rank = jnp.sum(jnp.where(span_ids == block_index, span_order, 0))
        allowed = (source_rank <= my_rank) & (linked | (block_index == my_span))
        valid = allowed & (slot_index < source_count)
        running_max, running_sum, accum = running
        scores = (
            jnp.einsum("qhd,khd->hqk", queries, key_block, preferred_element_type=jnp.float32)
            * score_factor
        )
        scores = jnp.where(valid[None, None, :], scores, NEG_FILL)
        new_max = jnp.maximum(running_max, jnp.max(scores, axis=-1))
        weights = jnp.where(valid[None, None, :], jnp.exp(scores - new_max[:, :, None]), 0.0)
        factor = jnp.exp(running_max - new_max)
        new_sum = running_sum * factor + jnp.sum(weights, axis=-1)
        new_accum = accum * factor[:, :, None] + jnp.einsum(
            "hqk,khd->hqd",
            weights.astype(jnp.bfloat16),
            value_block,
            preferred_element_type=jnp.float32,
        )
        return ((new_max, new_sum, new_accum), None)

    blocks = (key_blocks, value_blocks, jnp.arange(block_count, dtype=jnp.int32))
    result, unused = lax.scan(fold_block, initial, blocks)
    running_max, running_sum, accum = result
    attended = (accum / running_sum[:, :, None]).astype(jnp.bfloat16)
    attended = jnp.transpose(attended, (1, 0, 2)).reshape(row_count, head_local * HEAD_DIM)
    partial_out = jnp.dot(attended, w_out, preferred_element_type=jnp.float32)
    projected = lax.psum_scatter(
        partial_out.astype(jnp.bfloat16), "tensor", scatter_dimension=1, tiled=True
    ).astype(jnp.float32)
    gate_part = lax.dynamic_slice_in_dim(gate_row, column_start, shard_width)
    return (latents.astype(jnp.float32) + gate_part * projected).astype(jnp.bfloat16)


def solution(mesh):
    return jax.shard_map(
        on_device,
        mesh=mesh,
        in_specs=(
            P("frame", "tensor"),
            P(None, "tensor"),
            P(None, "tensor"),
            P(None, "tensor"),
            P("tensor", None),
            P("tensor", None),
            P("tensor", None),
            P(),
            P("frame"),
            P(),
            P("frame", None),
            P(),
        ),
        out_specs=P("frame", "tensor"),
        check_vma=False,
    )
```

profile of v0, /device:TPU:0, one launch (start us, length us, event | category | flops | bytes accessed | tf_op | source)
XLA Modules:
  0.0 428.1 jit_solution(2990120822217263245)
XLA Ops:
  8.0 1.5 select_reduce_fusion.3
  9.5 38.7 %all-gather.3.cloned.1.call-done = bf16[512,5120]{1,0:T(8,128)(2,1)} async-done(((bf16[512,640]{1,0:T(8,128)(2,1)}), bf16[512,5120]{1,0:T(8,128)(2,1)}) %all-gather.3.cloned.1.call-update) | async-done | bytes 5242896 | tf_op jit(solution)/shard_map/all_gather | solution.py:36
  48.2 4.2 convert_reduce_fusion
  52.4 3.0 fusion.28
  55.5 2.2 fusion.30
  58.1 1.4 copy-done.9
  59.5 2.2 fusion.36
  63.9 5.9 %fusion.37 = f32[512,384]{0,1:T(8,128)S(1)} fusion(bf16[512,5120]{1,0:T(8,128)(2,1)} %copy-done.1, bf16[5120,384]{1,0:T(8,128)(2,1)} %param.15), kind=kOutput, calls=%fused_computation.65 | convolution fusion | flops 2013265920 | bytes 9961472 | tf_op jit(solution)/shard_map/dot_general | solution.py:48
  70.5 90.9 %all-gather.5.cloned.1.call-done = bf16[2,8192,384]{1,2,0:T(8,128)(2,1)} async-done(((bf16[2,512,384]{1,2,0:T(8,128)(2,1)}), bf16[2,8192,384]{1,2,0:T(8,128)(2,1)}) %all-gather.5.cloned.1.call-update) | async-done | bytes 12582928 | tf_op jit(solution)/shard_map/all_gather | solution.py:72
  161.4 8.2 %fusion.34 = (bf16[1,8192,384]{1,2,0:T(8,128)(2,1)S(1)}, bf16[1,8192,384]{1,2,0:T(8,128)(2,1)}) fusion(bf16[2,8192,384]{1,2,0:T(8,128)(2,1)} %all-gather.5.cloned.1.call-done), kind=kLoop, calls=%fused_computation.62 | loop fusion | bytes 25165824 | tf_op jit(solution)/shard_map/slice | solution.py:75
  169.6 5.6 %copy.35 = bf16[48,8,16,512]{3,2,1,0:T(8,128)(2,1)} copy(bf16[48,8,16,512]{3,1,2,0:T(8,128)(2,1)S(1)} %bitcast.83) | data formatting | bytes 12582912
  175.1 9.1 %copy.28 = bf16[16,512,3,128]{3,1,2,0:T(8,128)(2,1)} copy(bf16[16,512,3,128]{1,0,3,2:T(8,128)(2,1)} %bitcast.80) | data formatting | bytes 12582912
  184.3 8.3 %copy.34 = bf16[48,8,16,512]{3,2,1,0:T(8,128)(2,1)} copy(bf16[48,8,16,512]{3,1,2,0:T(8,128)(2,1)} %bitcast.82) | data formatting | bytes 12582912
  192.6 9.2 %copy.27 = bf16[16,512,3,128]{3,1,2,0:T(8,128)(2,1)} copy(bf16[16,512,3,128]{1,0,3,2:T(8,128)(2,1)} %bitcast.81) | data formatting | bytes 12582912
  201.8 162.4 %while.17 = (s32[]{:T(128)}, f32[3,512]{1,0:T(4,128)S(1)}, f32[3,512]{1,0:T(4,128)S(1)}, f32[3,512,128]{2,1,0:T(8,128)S(1)}, s32[16]{0:T(128)S(1)}, /*index=5*/s...) while((s32[]{:T(128)}, f32[3,512]{1,0:T(4,128)S(1)}, ...), condition=%wide.region_12.13_spmd.clone.clone, body=%wide.region_6.12_spmd.clone.clone.sunk | while | flops 413475456 | bytes 12295147 | solution.py:103
  203.0 1.3 select_reduce_fusion.5
  206.9 1.6 bitcast_reduce_fusion.2
  209.4 2.4 fusion.60
  213.2 1.3 select_reduce_fusion.5
  217.1 1.6 bitcast_reduce_fusion.2
  219.6 2.4 fusion.60
  223.3 1.3 select_reduce_fusion.5
  227.2 1.6 bitcast_reduce_fusion.2
  229.7 2.4 fusion.60
  237.4 1.6 bitcast_reduce_fusion.2
  239.9 2.4 fusion.60
  243.6 1.3 select_reduce_fusion.5
  247.5 1.6 bitcast_reduce_fusion.2
  250.0 2.4 fusion.60
  253.7 1.3 select_reduce_fusion.5
  257.7 1.6 bitcast_reduce_fusion.2
  260.2 2.4 fusion.60
  263.9 1.3 select_reduce_fusion.5
  267.8 1.6 bitcast_reduce_fusion.2
  270.3 2.4 fusion.60
  274.0 1.3 select_reduce_fusion.5
  277.9 1.6 bitcast_reduce_fusion.2
  280.5 2.4 fusion.60
  284.2 1.3 select_reduce_fusion.5
  288.1 1.6 bitcast_reduce_fusion.2
  290.6 2.4 fusion.60
  294.3 1.3 select_reduce_fusion.5
  298.2 1.6 bitcast_reduce_fusion.2
  300.8 2.4 fusion.60
  308.4 1.6 bitcast_reduce_fusion.2
  310.9 2.4 fusion.60
  314.6 1.3 select_reduce_fusion.5
  318.5 1.6 bitcast_reduce_fusion.2
  321.1 2.4 fusion.60
  324.8 1.3 select_reduce_fusion.5
  328.7 1.6 bitcast_reduce_fusion.2
  331.2 2.4 fusion.60
  334.9 1.3 select_reduce_fusion.5
  338.8 1.6 bitcast_reduce_fusion.2
  341.4 2.4 fusion.60
  345.1 1.3 select_reduce_fusion.5
  349.0 1.6 bitcast_reduce_fusion.2
  351.5 2.4 fusion.60
  359.1 1.6 bitcast_reduce_fusion.2
  361.7 2.4 fusion.60
  364.5 6.8 %convolution_convert_fusion = bf16[512,5120]{1,0:T(8,128)(2,1)} fusion(bf16[512,384]{0,1:T(8,128)(2,1)S(1)} %bitcast.87, bf16[384,5120]{1,0:T(8,128)(2,1)} %param.18), kind=kOutput, calls=%fused_computation.41 | convolution fusion | flops 2015887360 | bytes 9568256 | tf_op jit(solution)/shard_map/dot_general | solution.py:107
  371.3 7.9 %copy.32 = bf16[512,5120]{0,1:T(8,128)(2,1)} copy(bf16[512,5120]{1,0:T(8,128)(2,1)} %convolution_convert_fusion) | data formatting | bytes 10485760
  379.3 39.8 %reduce-scatter.4.cloned.1.call-done = bf16[640,512]{1,0:T(8,128)(2,1)} async-done(((bf16[5120,512]{1,0:T(8,128)(2,1)}), bf16[640,512]{1,0:T(8,128)(2,1)}) %reduce-scatter.4.cloned.1.call-update) | async-done | bytes 655376
  419.1 1.4 copy.33
  (144 shorter events, 43.8 us)
Async XLA Ops:
  6.5 41.6 %all-gather.3.cloned.1.call-start = ((), (), s32[]{:S(2)}) async-start(), calls=%async_computation.1 | async-start | bytes 5898240 | tf_op jit(solution)/shard_map/all_gather | solution.py:36
  7.3 154.1 %all-gather.5.cloned.1.call-start = ((), (), s32[]{:S(2)}) async-start(), calls=%async_computation.2 | async-start | bytes 13369344 | tf_op jit(solution)/shard_map/all_gather | solution.py:72
  48.2 4.2 copy-start
  52.4 3.0 copy-start.8
  55.5 2.7 copy-start.1
  55.5 4.0 copy-start.9
  59.5 2.3 copy-start.6
  61.7 1.5 copy-start.3
  63.0 356.1 %reduce-scatter.4.cloned.1.call-start = ((), (), s32[]{:S(2)}) async-start(), calls=%async_computation.3 | async-start | bytes 5898240
  63.9 6.3 %copy-start.7 = (f32[3,128]{1,0:T(4,128)S(1)}, f32[3,128]{1,0:T(4,128)}, u32[]{:S(2)}) copy-start(f32[3,128]{1,0:T(4,128)} %param.19) | copy-start | bytes 4612
  192.6 9.2 %copy-start.4 = (s32[1,16]{1,0:T(1,128)S(1)}, s32[1,16]{1,0:T(1,128)}, u32[]{:S(2)}) copy-start(s32[1,16]{1,0:T(1,128)} %param.24) | copy-start | bytes 196
  192.6 9.2 %copy-start.5 = (s32[16]{0:T(128)S(1)}, s32[16]{0:T(128)}, u32[]{:S(2)}) copy-start(s32[16]{0:T(128)} %param.23) | copy-start | bytes 196
  379.3 41.2 %copy-start.2 = (bf16[512,640]{1,0:T(8,128)(2,1)S(1)}, bf16[512,640]{1,0:T(8,128)(2,1)}, u32[]{:S(2)}) copy-start(bf16[512,640]{1,0:T(8,128)(2,1)} %param.14) | copy-start | bytes 1966084
Sparse Core Ops, SparseCore 0:
  9.0 39.1 all-gather.2
  63.1 98.1 all-gather.4
  379.4 39.6 reduce-scatter.3
where the time goes:
time: 431 us; the launch traced here: 428 us
  waiting for transfers between devices  170 us (39%)
  matrix products  82 us (19%)
  local copies, waits for them, and re-layouts  61.9 us (14%)
  other arithmetic  58.1 us (13%)
  loops' own time  41.6 us (10%)
  between operations  14 us (3%)
    all_gather x1, waiting for transfers between devices, on_device(): piece = lax.all_gather(kv_pair, 'frame', axis=1, tiled=True)  90.9 us
    unnamed x26, local copies, waits for them, and re-layouts  43.3 us
    another operation x1, loops' own time, on_device(): result, unused = lax.scan(fold_block, initial, blocks)  41.6 us
    unnamed x4, waiting for transfers between devices  40.6 us
    dot_general x16, matrix products, fold_block(): jnp.einsum('hqk,khd->hqd', weights.astype(jnp.bfloat16), value_block, pre...  39.2 us
    all_gather x1, waiting for transfers between devices, on_device(): lax.all_gather(latents, 'tensor', axis=1, tiled=True).astype(jnp.float32)  38.7 us
    dot_general x16, matrix products, fold_block(): jnp.einsum('qhd,khd->hqk', queries, key_block, preferred_element_type=jnp...  25.6 us
    reduce_sum x16, other arithmetic, fold_block(): linked = jnp.sum(jnp.where(span_ids == block_index, mask_row, 0)) == 1  21.5 us
  transfers between devices with their start and end apart: 3, of which 3 were waited for; matrix products, arithmetic and copies ran while one was open for 2% of the time, Pallas kernels for 0%

commit v1 on v0

--- a/solution.py
+++ b/solution.py
@@ -33,7 +33,9 @@
     shift_row = modulation[0]
     scale_row = modulation[1]
     gate_row = modulation[2]
-    whole = lax.all_gather(latents, "tensor", axis=1, tiled=True).astype(jnp.float32)
+    whole = jnp.concatenate(
+        lax.all_to_all(jnp.stack([latents] * lax.axis_size("tensor")), "tensor", 0, 0), axis=1
+    ).astype(jnp.float32)
     row_mean = jnp.mean(whole, axis=1, keepdims=True)
     row_square = jnp.mean(whole * whole, axis=1, keepdims=True)
     normed = (

time: 431 us -> 482 us (1.12)
  local copies, waits for them, and re-layouts: 61.9 us -> 104 us
  starting transfers between devices: 0.26 us -> 5.82 us
    all_to_all x0 -> x1, waiting for transfers between devices: none -> 53.5 us  [on_device(): lax.all_to_all(jnp.stack([latents] * lax.axis_size('tensor')), 'tensor',...]
    all_gather x1 -> x0, waiting for transfers between devices: 38.7 us -> none  [on_device(): lax.all_gather(latents, 'tensor', axis=1, tiled=True).astype(jnp.float32)]
    another operation x0 -> x4, local copies, waits for them, and re-layouts: none -> 37.3 us  [the longest x1 16.6 us: on_device(): key_blocks = piece[0].reshape(block_count, row_count, head_local, HEAD_DIM)]
    all_gather x1, waiting for transfers between devices: 90.9 us -> 75.2 us  [on_device(): piece = lax.all_gather(kv_pair, 'frame', axis=1, tiled=True)]
    all_to_all x0 -> x1, local copies, waits for them, and re-layouts: none -> 7.86 us  [on_device(): lax.all_to_all(jnp.stack([latents] * lax.axis_size('tensor')), 'tensor',...]
    all_to_all x0 -> x1, starting transfers between devices: none -> 5.56 us  [on_device(): lax.all_to_all(jnp.stack([latents] * lax.axis_size('tensor')), 'tensor',...]
    unnamed x26 -> x29, local copies, waits for them, and re-layouts: 43.3 us -> 37.9 us
    unnamed x4 -> x3, waiting for transfers between devices: 40.6 us -> 40.1 us
  transfers between devices with their start and end apart: 3 -> 3, of which waited for: 3 -> 3; matrix products, arithmetic and copies ran while one was open for 2% -> 4% of each run, Pallas kernels for 0% -> 0%
where the time goes in v1:
time: 482 us; the launch traced here: 478 us
  waiting for transfers between devices  169 us (35%)
  local copies, waits for them, and re-layouts  104 us (22%)
  matrix products  83.2 us (17%)
  other arithmetic  59.9 us (12%)
  loops' own time  42.4 us (9%)
  between operations  14.3 us (3%)
  starting transfers between devices  5.82 us (1%)
    all_gather x1, waiting for transfers between devices, on_device(): piece = lax.all_gather(kv_pair, 'frame', axis=1, tiled=True)  75.2 us
    all_to_all x1, waiting for transfers between devices, on_device(): lax.all_to_all(jnp.stack([latents] * lax.axis_size('tensor')), 'tensor',...  53.5 us
    another operation x1, loops' own time, on_device(): result, unused = lax.scan(fold_block, initial, blocks)  42.4 us
    unnamed x3, waiting for transfers between devices  40.1 us
    dot_general x16, matrix products, fold_block(): jnp.einsum('hqk,khd->hqd', weights.astype(jnp.bfloat16), value_block, pre...  39.2 us
    unnamed x29, local copies, waits for them, and re-layouts  37.9 us
    dot_general x16, matrix products, fold_block(): jnp.einsum('qhd,khd->hqk', queries, key_block, preferred_element_type=jnp...  25.6 us
    reduce_sum x16, other arithmetic, fold_block(): linked = jnp.sum(jnp.where(span_ids == block_index, mask_row, 0)) == 1  21.5 us
  transfers between devices with their start and end apart: 3, of which 3 were waited for; matrix products, arithmetic and copies ran while one was open for 4% of the time, Pallas kernels for 0%

profile of v1, /device:TPU:0, one launch (start us, length us, event | category | flops | bytes accessed | tf_op | source)
XLA Modules:
  0.0 478.1 jit_solution(4562683713648952394)
XLA Ops:
  6.5 3.8 stack.6
  10.4 5.6 %all-to-all-start = ((bf16[8,512,640]{2,1,0:T(8,128)(2,1)}), bf16[8,512,640]{2,1,0:T(8,128)(2,1)}, u32[]{:S(2)}, u32[]{:S(2)}) async-start(bf16[8,512,640]{2,1,0:T(8,128)(2,1)} %stack.6), calls=%async_computation | async-start | bytes 10485760 | tf_op jit(solution)/shard_map/all_to_all | solution.py:37
  17.1 6.3 %copy.42 = bf16[5120,384]{0,1:T(8,128)(2,1)} copy(bf16[5120,384]{1,0:T(8,128)(2,1)} %param.16) | data formatting | bytes 7864320 | tf_op args[2]
  23.4 53.5 %all-to-all-done = bf16[8,512,640]{2,1,0:T(8,128)(2,1)} async-done(((bf16[8,512,640]{2,1,0:T(8,128)(2,1)}), bf16[8,512,640]{2,1,0:T(8,128)(2,1)}, u32[]{:S(2)}, u32[]{:S(2)}) %all-to-all-start) | async-done | bytes 5242912 | tf_op jit(solution)/shard_map/all_to_all | solution.py:37
  76.9 7.9 %copy.41 = bf16[8,512,640]{1,2,0:T(8,128)(2,1)} copy(bf16[8,512,640]{2,1,0:T(8,128)(2,1)} %all-to-all-done) | data formatting | bytes 10485760 | tf_op jit(solution)/shard_map/all_to_all | solution.py:37
  84.8 4.0 convert_reduce_fusion
  88.9 2.2 add_convert_fusion
  91.1 2.2 multiply_reduce_fusion.2
  93.7 5.1 %fusion.28 = bf16[512,5120]{0,1:T(8,128)(2,1)S(1)} fusion(bf16[8,512,640]{1,2,0:T(8,128)(2,1)} %copy.41, f32[5120]{0:T(1024)S(1)} %bitcast.91, f32[5120]{0:T(1024)S(1)} %bitcast.92, f32[512]{0:T(512)S(1)} %get-tuple-element.288, f32[512]{0:T(512)S(1)} %get-tuple-element.287), kind=kLoop, calls=%fused_computation.37 | loop fusion | flops 15728640 | bytes 10530816 | tf_op jit(solution)/shard_map/convert_element_type | solution.py:46
  98.8 2.9 fusion.29
  103.0 6.3 %copy.46 = bf16[5120,384]{0,1:T(8,128)(2,1)} copy(bf16[5120,384]{1,0:T(8,128)(2,1)} %param.15) | data formatting | bytes 7864320 | tf_op args[1]
  110.0 6.5 %multiply_reduce_fusion.1 = (f32[512,3]{0,1:T(4,128)S(1)}, f32[512,3,128]{0,2,1:T(8,128)S(1)}) fusion(bf16[512,5120,1]{0,1,2:T(8,128)(2,1)} %bitcast.85, bf16[3,128,5120]{2,1,0:T(8,128)(2,1)} %bitcast.87), kind=kOutput, calls=%fused_computation.49 | convolution fusion | flops 2013657600 | bytes 9967616 | tf_op jit(solution)/shard_map/dot_general | solution.py:50
  116.9 75.2 %all-gather.2.cloned.1.call-done = bf16[2,8192,384]{2,1,0:T(8,128)(2,1)} async-done(((bf16[2,512,384]{2,1,0:T(8,128)(2,1)}), bf16[2,8192,384]{2,1,0:T(8,128)(2,1)}) %all-gather.2.cloned.1.call-update) | async-done | bytes 12582928 | tf_op jit(solution)/shard_map/all_gather | solution.py:74
  192.1 10.4 %fusion.32 = (bf16[1,8192,384]{2,1,0:T(8,128)(2,1)}, bf16[1,8192,384]{2,1,0:T(8,128)(2,1)}) fusion(bf16[2,8192,384]{2,1,0:T(8,128)(2,1)} %all-gather.2.cloned.1.call-done), kind=kLoop, calls=%fused_computation.63 | loop fusion | bytes 25165824 | tf_op jit(solution)/shard_map/slice | solution.py:77
  202.5 16.6 %reshape.109 = bf16[16,512,3,128]{3,2,1,0:T(4,128)(2,1)} reshape(bf16[1,8192,384]{2,1,0:T(8,128)(2,1)} %get-tuple-element.282) | data formatting | bytes 12582912 | tf_op jit(solution)/shard_map/reshape;squeeze | solution.py:77
  219.1 7.9 %copy.51 = bf16[16,512,3,128]{3,1,2,0:T(8,128)(2,1)} copy(bf16[16,512,3,128]{3,2,1,0:T(4,128)(2,1)} %reshape.109) | data formatting | bytes 12582912
  227.0 16.6 %reshape.108 = bf16[16,512,3,128]{3,2,1,0:T(4,128)(2,1)} reshape(bf16[1,8192,384]{2,1,0:T(8,128)(2,1)} %get-tuple-element.283) | data formatting | bytes 12582912 | tf_op jit(solution)/shard_map/reshape;squeeze | solution.py:76
  243.6 7.7 %copy.49 = bf16[16,512,3,128]{3,1,2,0:T(8,128)(2,1)} copy(bf16[16,512,3,128]{3,2,1,0:T(4,128)(2,1)} %reshape.108) | data formatting | bytes 12582912
  251.4 162.2 %while.17 = (s32[]{:T(128)}, f32[3,512]{1,0:T(4,128)S(1)}, f32[3,512]{1,0:T(4,128)S(1)}, f32[3,512,128]{2,1,0:T(8,128)S(1)}, s32[16]{0:T(128)S(1)}, /*index=5*/s...) while((s32[]{:T(128)}, f32[3,512]{1,0:T(4,128)S(1)}, ...), condition=%wide.region_12.13_spmd.clone.clone, body=%wide.region_6.12_spmd.clone.clone.sunk | while | flops 413475456 | bytes 12295147 | solution.py:105
  252.6 1.3 select_reduce_fusion.5
  256.5 1.6 bitcast_reduce_fusion.2
  259.0 2.4 fusion.55
  266.6 1.6 bitcast_reduce_fusion.2
  269.2 2.4 fusion.55
  272.9 1.3 select_reduce_fusion.5
  276.8 1.6 bitcast_reduce_fusion.2
  279.3 2.4 fusion.55
  283.0 1.3 select_reduce_fusion.5
  286.9 1.6 bitcast_reduce_fusion.2
  289.4 2.4 fusion.55
  293.2 1.3 select_reduce_fusion.5
  297.1 1.6 bitcast_reduce_fusion.2
  299.6 2.4 fusion.55
  303.3 1.3 select_reduce_fusion.5
  307.2 1.6 bitcast_reduce_fusion.2
  309.7 2.4 fusion.55
  317.3 1.6 bitcast_reduce_fusion.2
  319.9 2.4 fusion.55
  327.5 1.6 bitcast_reduce_fusion.2
  330.0 2.4 fusion.55
  337.6 1.6 bitcast_reduce_fusion.2
  340.1 2.4 fusion.55
  347.8 1.6 bitcast_reduce_fusion.2
  350.3 2.4 fusion.55
  354.0 1.3 select_reduce_fusion.5
  357.9 1.6 bitcast_reduce_fusion.2
  360.4 2.4 fusion.55
  364.1 1.3 select_reduce_fusion.5
  368.0 1.6 bitcast_reduce_fusion.2
  370.6 2.4 fusion.55
  374.3 1.3 select_reduce_fusion.5
  378.2 1.6 bitcast_reduce_fusion.2
  380.7 2.4 fusion.55
  384.4 1.3 select_reduce_fusion.5
  388.3 1.6 bitcast_reduce_fusion.2
  390.8 2.4 fusion.55
  398.5 1.6 bitcast_reduce_fusion.2
  401.0 2.4 fusion.55
  408.6 1.6 bitcast_reduce_fusion.2
  411.1 2.4 fusion.55
  414.0 6.8 %convolution_convert_fusion = bf16[512,5120]{1,0:T(8,128)(2,1)} fusion(bf16[512,384]{0,1:T(8,128)(2,1)S(1)} %bitcast.88, bf16[384,5120]{1,0:T(8,128)(2,1)} %param.18), kind=kOutput, calls=%fused_computation.41 | convolution fusion | flops 2015887360 | bytes 9568256 | tf_op jit(solution)/shard_map/dot_general | solution.py:109
  420.8 7.9 %copy.62 = bf16[512,5120]{0,1:T(8,128)(2,1)} copy(bf16[512,5120]{1,0:T(8,128)(2,1)} %convolution_convert_fusion) | data formatting | bytes 10485760
  428.8 40.0 %reduce-scatter.4.cloned.1.call-done = bf16[640,512]{1,0:T(8,128)(2,1)} async-done(((bf16[5120,512]{1,0:T(8,128)(2,1)}), bf16[640,512]{1,0:T(8,128)(2,1)}) %reduce-scatter.4.cloned.1.call-update) | async-done | bytes 655376
  468.8 1.4 copy.63
  (151 shorter events, 47.6 us)
Async XLA Ops:
  10.4 6.3 %copy-start.5 = (f32[16,3,5120]{2,0,1:T(8,128)S(1)}, f32[16,3,5120]{2,0,1:T(8,128)}, u32[]{:S(2)}) copy-start(f32[16,3,5120]{2,0,1:T(8,128)} %param.21) | copy-start | bytes 2949124
  10.4 66.5 %all-to-all-start = ((bf16[8,512,640]{2,1,0:T(8,128)(2,1)}), bf16[8,512,640]{2,1,0:T(8,128)(2,1)}, u32[]{:S(2)}, u32[]{:S(2)}) async-start(bf16[8,512,640]{2,1,0:T(8,128)(2,1)} %stack.6), calls=%async_computation | async-start | bytes 10485760 | tf_op jit(solution)/shard_map/all_to_all | solution.py:37
  15.9 176.1 %all-gather.2.cloned.1.call-start = ((), (), s32[]{:S(2)}) async-start(), calls=%async_computation.2 | async-start | bytes 13369344 | tf_op jit(solution)/shard_map/all_gather | solution.py:74
  84.8 4.1 copy-start
  88.8 2.2 copy-start.3
  91.0 2.3 copy-start.2
  91.1 2.3 copy-start.9
  93.7 5.1 %copy-start.1 = (bf16[5120,384]{1,0:T(8,128)(2,1)S(1)}, bf16[5120,384]{1,0:T(8,128)(2,1)}, u32[]{:S(2)}) copy-start(bf16[5120,384]{1,0:T(8,128)(2,1)} %param.17) | copy-start | bytes 11796484
  101.7 7.6 %copy-start.6 = (s32[16]{0:T(128)S(1)}, s32[16]{0:T(128)}, u32[]{:S(2)}) copy-start(s32[16]{0:T(128)} %param.25) | copy-start | bytes 196
  102.8 366.1 %reduce-scatter.4.cloned.1.call-start = ((), (), s32[]{:S(2)}) async-start(), calls=%async_computation.3 | async-start | bytes 5898240
  110.0 6.5 %copy-start.10 = (f32[3,128]{1,0:T(4,128)S(1)}, f32[3,128]{1,0:T(4,128)}, u32[]{:S(2)}) copy-start(f32[3,128]{1,0:T(4,128)} %param.19) | copy-start | bytes 4612
  243.6 7.8 %copy-start.7 = (s32[1,16]{1,0:T(1,128)S(1)}, s32[1,16]{1,0:T(1,128)}, u32[]{:S(2)}) copy-start(s32[1,16]{1,0:T(1,128)} %param.24) | copy-start | bytes 196
  243.6 7.8 %copy-start.8 = (s32[16]{0:T(128)S(1)}, s32[16]{0:T(128)}, u32[]{:S(2)}) copy-start(s32[16]{0:T(128)} %param.23) | copy-start | bytes 196
  428.7 41.5 %copy-start.4 = (bf16[512,640]{1,0:T(8,128)(2,1)S(1)}, bf16[512,640]{1,0:T(8,128)(2,1)}, u32[]{:S(2)}) copy-start(bf16[512,640]{1,0:T(8,128)(2,1)} %param.14) | copy-start | bytes 1966084
Sparse Core Ops, SparseCore 0:
  102.9 89.1 all-gather.1
  428.9 39.8 reduce-scatter.3
